TPU v7x, 32 devices: a whole 2x2x4 slice. The times are simulated.
32 devices in a mesh: sensor: 4 (over y, core), space: 8 (over z, x).
Axes of the slice: x: 2, y: 2, z: 4, core: 2. Of those that a mesh axis runs over, the one named last changes fastest.
Arguments:
- jacobian: float32 [512, 16384], P('space', 'sensor'), as said below
- residual: float32 [16384], P('sensor'), may hold values from -6 to 6
- damping: float32 [1], replicated, may hold values from 0.3 to 3
Outputs:
- update: float32 [512], replicated
Inputs may be any that keep to these rules, and one draw needn't show every extreme that they name: `jacobian`: every column block of the Jacobian has full rank over any 512 observations, which number at least the parameters; the entries are real-valued with row and column scales that vary.
All inputs are finite; a program needn't handle non-finite values.
Results may differ from a plain program's by a relative error of at most 0.00011.
Values sent between devices are 32-bit elements; how exact they have to be, the bound alone decides.
No kernel may reach another device: no remote copies, remote signals or barrier semaphores. Data moves between devices by JAX's collectives and lax.ppermute only.
A program may use at most 64 MiB of HBM per device.

v0:
```python
import jax
import jax.numpy as jnp
from jax import lax
from jax.sharding import PartitionSpec as P


def per_device(jacobian, residual, damping):
    high = lax.Precision.HIGHEST
    columns = jacobian.shape[0]
    groups = lax.axis_size("space")
    params_all = columns * groups
    part_grad = jnp.dot(jacobian, residual, precision=high)
    grad_local = lax.dynamic_update_slice(
        jnp.zeros((params_all,), jnp.float32), part_grad, (lax.axis_index("space") * columns,)
    )
    panel_t = lax.all_to_all(jacobian, "space", split_axis=1, concat_axis=0, tiled=True)
    gram_local = lax.dot_general(panel_t, panel_t, (((1,), (1,)), ((), ())), precision=high)
    gram_group, grad_group = lax.psum((gram_local, grad_local), "space")
    gram_all, grad_all = lax.psum((gram_group, grad_group), "sensor")
    damped = gram_all + damping[0] * jnp.diag(jnp.diag(gram_all))
    factor = jnp.linalg.cholesky(damped)
    return -jax.scipy.linalg.cho_solve((factor, True), grad_all)


def solution(mesh):
    placed = (P("space", "sensor"), P("sensor"), P())
    return jax.shard_map(per_device, mesh=mesh, in_specs=placed, out_specs=P(), check_vma=False)
```

profile of v0, /device:TPU:0, one launch (start us, length us, event | category | flops | bytes accessed | tf_op | source)
XLA Modules:
  0.0 311.7 jit_solution(12249171158985935714)
XLA Ops:
  6.5 1.3 copy.52
  7.9 32.8 %all_to_all.19 = f32[64,8,512]{2,0,1:T(8,128)S(1)} all-to-all(f32[64,8,512]{2,0,1:T(8,128)S(1)} %bitcast.158), channel_id=1, replica_groups=mesh['sensor'=4,'space'=8] {'space'}, dimensions={1} | all-to-all | bytes 2097152 | tf_op jit(solution)/shard_map/all_to_all | solution.py:16
  40.7 2.9 fusion.57
  43.7 77.3 %all-reduce.4.cloned.1.call-done = f32[512,512]{0,1:T(8,128)} async-done(((f32[512,512]{0,1:T(8,128)}), f32[512,512]{0,1:T(8,128)}) %all-reduce.4.cloned.1.call-update) | async-done | bytes 1048592 | tf_op jit(solution)/shard_map/psum | solution.py:18
  121.7 0.9 convolution_bitcast_fusion
  122.8 20.0 %psum.30 = f32[512]{0:T(512)S(1)} all-reduce(f32[512]{0:T(512)S(1)} %dynamic_update_slice.3), channel_id=1, replica_groups=mesh['sensor'=4,'space'=8] {'space'}, use_global_device_ids=true, to_apply=%region_10.11 | all-reduce | flops 512 | bytes 4096 | tf_op jit(solution)/shard_map/psum | solution.py:18
  142.8 5.6 %psum.31 = f32[512]{0:T(512)S(1)} all-reduce(f32[512]{0:T(512)S(1)} %psum.30), channel_id=1, replica_groups=mesh['sensor'=4,'space'=8] {'sensor'}, use_global_device_ids=true, to_apply=%region_11.12 | all-reduce | flops 512 | bytes 4096 | tf_op jit(solution)/shard_map/psum | solution.py:19
  148.5 10.8 %all-reduce.6.cloned.1.call-done = f32[512,512]{0,1:T(8,128)} async-done(((f32[512,512]{0,1:T(8,128)}), f32[512,512]{0,1:T(8,128)}) %all-reduce.6.cloned.1.call-update) | async-done | bytes 1048592 | tf_op jit(solution)/shard_map/psum | solution.py:19
  159.3 8.7 %gather_fusion = f32[512]{0:T(512)S(1)} fusion(f32[512,512]{0,1:T(8,128)} %all-reduce.6.cloned.1.call-done, s32[512]{0:T(512)S(1)} %bitcast.155), kind=kCustom, calls=%fused_computation | custom fusion | bytes 8192 | tf_op jit(solution)/shard_map/jit(_diag)/jit(diagonal)/cond/branch_0_fun/gather | solution.py:20
  168.7 11.7 %cholesky.103 = f32[128,128]{1,0:T(8,128)S(1)} custom-call(f32[128,128]{1,0:T(8,128)S(1)} %cholesky.263), custom_call_target="Cholesky" | custom-call | tf_op jit(solution)/shard_map/jit(cholesky)/cholesky | solution.py:21
  180.6 9.8 %custom-call.34 = f32[1,128,128]{1,2,0:T(8,128)S(1)} custom-call(f32[1,128,128]{2,1,0:T(8,128)S(1)} %get-tuple-element.44), custom_call_target="InvertDiagBlocksLowerTriangular" | custom-call | tf_op jit(solution)/shard_map/jit(cholesky)/cholesky | solution.py:21
  191.2 11.7 %cholesky.215 = f32[128,128]{1,0:T(8,128)S(1)} custom-call(f32[128,128]{1,0:T(8,128)S(1)} %cholesky.267), custom_call_target="Cholesky" | custom-call | tf_op jit(solution)/shard_map/jit(cholesky)/cholesky | solution.py:21
  203.2 10.0 %custom-call.35 = f32[1,128,128]{1,2,0:T(8,128)S(1)} custom-call(f32[1,128,128]{2,1,0:T(8,128)S(1)} %get-tuple-element.42), custom_call_target="InvertDiagBlocksLowerTriangular" | custom-call | tf_op jit(solution)/shard_map/jit(cholesky)/cholesky | solution.py:21
  214.1 11.7 %cholesky.236 = f32[128,128]{1,0:T(8,128)S(1)} custom-call(f32[128,128]{1,0:T(8,128)S(1)} %cholesky.272), custom_call_target="Cholesky" | custom-call | tf_op jit(solution)/shard_map/jit(cholesky)/cholesky | solution.py:21
  226.0 9.8 %custom-call.36 = f32[1,128,128]{1,2,0:T(8,128)S(1)} custom-call(f32[1,128,128]{2,1,0:T(8,128)S(1)} %get-tuple-element.40), custom_call_target="InvertDiagBlocksLowerTriangular" | custom-call | tf_op jit(solution)/shard_map/jit(cholesky)/cholesky | solution.py:21
  236.6 11.9 %cholesky.253 = f32[128,128]{1,0:T(8,128)S(1)} custom-call(f32[128,128]{1,0:T(8,128)S(1)} %convolution_subtract_fusion.2), custom_call_target="Cholesky" | custom-call | tf_op jit(solution)/shard_map/jit(cholesky)/cholesky | solution.py:21
  248.7 0.7 compare_reduce_fusion.1
  250.1 0.7 compare_reduce_fusion.2
  253.4 8.6 %while.1 = (s32[]{:T(128)}, f32[512,512]{0,1:T(8,128)S(1)}, s32[4,2]{0,1:T(2,128)S(1)}, f32[4,128,128]{2,1,0:T(8,128)S(1)}, s32[]{:T(128)}) while((s32[]{:T(128)}, f32[512,512]{0,1:T(8,128)S(1)}, s32[4,2]{0,1:T(2,128)S(1)}, f32[4,128,128]{2,1,0:T(8,128)S(1)}, s32[]{:T(128)}) %tuple.27), condition=%wide.while_cond, body=%wide.while_body.sunk | while | flops 2 | bytes 393329 | solution.py:22
  254.1 1.3 dynamic-slice.7
  256.3 1.3 dynamic-slice.7
  258.4 1.3 dynamic-slice.7
  260.6 1.3 dynamic-slice.7
  262.0 39.3 %custom-call.37 = f32[4,128,128]{1,2,0:T(8,128)S(1)} custom-call(f32[4,128,128]{2,1,0:T(8,128)S(1)} %get-tuple-element.12), custom_call_target="InvertDiagBlocksLowerTriangular" | custom-call | tf_op jit(solution)/shard_map/jit(_cho_solve)/triangular_solve | solution.py:22
  (75 shorter events, 11.6 us)
Async XLA Ops:
  6.5 115.1 %copy-start = (f32[4096]{0:T(1024)S(1)}, f32[4096]{0:T(1024)}, u32[]{:S(2)}) copy-start(f32[4096]{0:T(1024)} %param.4) | copy-start | bytes 49156
  6.5 114.4 %all-reduce.4.cloned.1.call-start = ((), (), s32[]{:S(2)}) async-start(), calls=%async_computation.1 | async-start | bytes 2097152 | tf_op jit(solution)/shard_map/psum | solution.py:18
  43.6 78.1 %copy-start.2 = (f32[64,4096]{1,0:T(8,128)S(1)}, f32[64,4096]{1,0:T(8,128)}, u32[]{:S(2)}) copy-start(f32[64,4096]{1,0:T(8,128)} %param.3) | copy-start | bytes 3145732
  43.6 115.6 %all-reduce.6.cloned.1.call-start = ((), (), s32[]{:S(2)}) async-start(), calls=%async_computation.2 | async-start | bytes 2097152 | tf_op jit(solution)/shard_map/psum | solution.py:19
  159.3 8.7 %copy-start.1 = (f32[512,512]{0,1:T(8,128)S(1)}, f32[512,512]{0,1:T(8,128)}, u32[]{:S(2)}) copy-start(f32[512,512]{0,1:T(8,128)} %all-reduce.6.cloned.1.call-done) | copy-start | bytes 3145732
Sparse Core Ops, SparseCore 0:
  43.8 77.1 all-reduce.3
  123.3 35.8 all-reduce.5
where the time goes:
time: 312 us
  other arithmetic  119 us (38%)
  waiting for transfers between devices  88.1 us (28%)
  blocking collectives  58.5 us (19%)
  local copies, waits for them, and re-layouts  19.7 us (6%)
  between operations  16.9 us (5%)
  matrix products  9.06 us (3%)
    another operation x14, other arithmetic, per_device(): factor = jnp.linalg.cholesky(damped)  78.9 us
    psum x1, waiting for transfers between devices, per_device(): gram_group, grad_group = lax.psum((gram_local, grad_local), 'space')  77.3 us
    another operation x3, other arithmetic, per_device(): return -jax.scipy.linalg.cho_solve((factor, True), grad_all)  39.4 us
    all_to_all x1, blocking collectives, per_device(): lax.all_to_all(jacobian, 'space', split_axis=1, concat_axis=0, tiled=True)  32.8 us
    psum x1, blocking collectives, per_device(): gram_group, grad_group = lax.psum((gram_local, grad_local), 'space')  20 us
    psum x1, waiting for transfers between devices, per_device(): gram_all, grad_all = lax.psum((gram_group, grad_group), 'sensor')  10.8 us
    gather x1, local copies, waits for them, and re-layouts, per_device(): damped = gram_all + damping[0] * jnp.diag(jnp.diag(gram_all))  8.67 us
    another operation x20, local copies, waits for them, and re-layouts  8.46 us
  transfers between devices with their start and end apart: 2, of which 2 were waited for; matrix products, arithmetic and copies ran while one was open for 0% of the time, Pallas kernels for 0%

commit v1 on v0

v1 whole, which is shorter than its diff:
```python
import functools

import jax
import jax.numpy as jnp
from jax import lax
from jax.experimental import pallas as pl
from jax.experimental.pallas import tpu as pltpu
from jax.sharding import PartitionSpec as P

B = 128
VMEM = pl.BlockSpec(memory_space=pltpu.VMEM)
SMEM = pl.BlockSpec(memory_space=pltpu.SMEM)


def f32(*shape):
    return jax.ShapeDtypeStruct(shape, jnp.float32)


def dot(a, b, dims=((1,), (0,))):
    return lax.dot_general(
        a, b, (dims, ((), ())), precision=lax.Precision.HIGHEST, preferred_element_type=jnp.float32
    )


def panel_starts(size):
    starts = [0]
    for k in range(size // B):
        starts.append(starts[-1] + size - k * B)
    return starts


def gram_kernel(order, total, *refs):
    residual_ref, own_ref, *got = refs[: len(order) + 2]
    keep_ref, send_ref, rows_ref, pack_ref = refs[len(order) + 2 :]
    me, core = lax.axis_index("space"), lax.rem(lax.axis_index("sensor"), 2)
    size = rows_ref.shape[0]
    part = own_ref.shape[0]
    for step, ref in zip([0] + order, [own_ref] + got):
        at = pl.multiple_of(jnp.bitwise_xor(me, step) * part, part)
        rows_ref[pl.ds(at, part), :] = ref[...]
    starts = panel_starts(size)
    for k in range(size // B):
        pack_ref[starts[k] : starts[k + 1], :] = dot(
            rows_ref[k * B :, :], rows_ref[k * B : (k + 1) * B, :], ((1,), (1,))
        )
    grad = dot(jnp.broadcast_to(residual_ref[...], (8, residual_ref.shape[1])), rows_ref[...], ((1,), (1,)))
    tail = starts[-1]
    pack_ref[tail:total, :] = jnp.zeros((total - tail, B), jnp.float32)
    for k in range(size // B):
        pack_ref[tail + k : tail + k + 1, :] = grad[0:1, k * B : (k + 1) * B]
    half = total // 2
    keep_ref[...] = pack_ref[pl.ds(pl.multiple_of(core * half, 8), half), :]
    send_ref[...] = pack_ref[pl.ds(pl.multiple_of((1 - core) * half, 8), half), :]


def plane_index():
    return lax.div(lax.axis_index("sensor"), 2) * 2 + lax.rem(lax.axis_index("space"), 2)


def split_kernel(keep_ref, got_ref, *refs):
    *outs, sum_ref = refs
    sum_ref[...] = keep_ref[...] + got_ref[...]
    me, part = plane_index(), outs[0].shape[0]
    for t, out in enumerate(outs):
        out[...] = sum_ref[pl.ds(pl.multiple_of(jnp.bitwise_xor(me, t) * part, part), part), :]


def join_kernel(*refs):
    *parts, out_ref = refs
    me, part = plane_index(), parts[0].shape[0]
    for t, ref in enumerate(parts):
        out_ref[pl.ds(pl.multiple_of(jnp.bitwise_xor(me, t) * part, part), part), :] = ref[...]


def lanes(x, l):
    return jnp.broadcast_to(x[:, l : l + 1], x.shape)


def subs(x, s):
    return jnp.broadcast_to(x[s : s + 1, :], x.shape)


def inverse(tiles, zero, width=16):
    tiles = list(tiles)
    n, h = len(tiles), width // 8
    lane = lax.broadcasted_iota(jnp.int32, tiles[0].shape, 1)
    sub = lax.broadcasted_iota(jnp.int32, tiles[0].shape, 0)
    for m in range(0, n, h):
        base = 8 * m
        rows = tiles[m : m + h]
        wide = [[lanes(rows[q], base + c) + zero for q in range(h)] for c in range(width)]
        for c in range(width):
            q0, s = divmod(c, 8)
            inv = 1.0 / subs(wide[c][q0], s)
            head = sub == s
            at = lane == base + c
            unit = jnp.where(head, 1.0, 0.0)
            rows = [jnp.where(at, unit if q == q0 else 0.0, rows[q]) for q in range(h)]
            for block in wide[c + 1 :] + [rows]:
                t = subs(block[q0], s) * inv
                for q in range(h):
                    rest = block[q] - wide[c][q] * t
                    block[q] = jnp.where(head, t, rest) if q == q0 else rest
        w = [subs(rows[c // 8], c % 8) for c in range(width)]
        keep = (lane < base) | (lane >= base + width)
        for i in list(range(m + h, n)) + list(range(m)):
            t = [lanes(tiles[i], base + c) * w[c] for c in range(width)]
            while len(t) > 1:
                t = [a + b for a, b in zip(t[::2], t[1::2])]
            tiles[i] = jnp.where(keep, tiles[i], 0.0) - t[0]
        tiles[m : m + h] = rows
    return tiles


def solve_kernel(size, damp_ref, mine_ref, other_ref, x_ref, pack_ref, d_ref, v_ref, *panels):
    nb = size // B
    w_refs, z_refs = panels[:nb], panels[nb:]
    core = lax.rem(lax.axis_index("sensor"), 2)
    half = mine_ref.shape[0]
    pack_ref[pl.ds(pl.multiple_of(core * half, 8), half), :] = mine_ref[...]
    pack_ref[pl.ds(pl.multiple_of((1 - core) * half, 8), half), :] = other_ref[...]
    starts = panel_starts(size)
    factor = damp_ref[0]
    zero = jnp.minimum(jnp.full((8, B), jnp.abs(factor)), 0.0)
    lane = lax.broadcasted_iota(jnp.int32, (8, B), 1)
    sub = lax.broadcasted_iota(jnp.int32, (8, B), 0)
    for k, w_ref in enumerate(w_refs):
        rows = size - k * B
        w_ref[0:rows, :] = pack_ref[starts[k] : starts[k + 1], :]
        w_ref[rows : rows + 8, :] = jnp.broadcast_to(pack_ref[starts[-1] + k : starts[-1] + k + 1, :], (8, B))
        for t in range(B // 8):
            a = w_ref[8 * t : 8 * t + 8, :]
            w_ref[8 * t : 8 * t + 8, :] = a + jnp.where(lane == sub + 8 * t, a * factor, 0.0)
    d_ref[...] = w_refs[0][0:B, :]

    def step(i, carry):
        inv = inverse([d_ref[8 * t : 8 * t + 8, :] for t in range(B // 8)], zero)
        for t in range(B // 8):
            v_ref[8 * t : 8 * t + 8, :] = inv[t]
        for k in range(nb):

            @pl.when(i == k)
            def _():
                z_refs[k][...] = dot(w_refs[k][B:, :], v_ref[...])
                for j in range(k + 1, nb):
                    at = (j - k) * B
                    new = w_refs[j][...] - dot(
                        z_refs[k][at - B :, :], w_refs[k][at : at + B, :], ((1,), (1,))
                    )
                    if j == k + 1:
                        d_ref[...] = new[0:B]
                    w_refs[j][...] = new

        return carry

    lax.fori_loop(0, nb, step, 0)
    x = [None] * nb
    for k in reversed(range(nb)):
        below = (nb - 1 - k) * B
        s = z_refs[k][below : below + 8, :]
        for j in range(k + 1, nb):
            s = s - dot(x[j], z_refs[k][(j - k - 1) * B : (j - k) * B, :])
        x[k] = s
        x_ref[0:1, k * B : (k + 1) * B] = -s[0:1]


def tree_sum(parts):
    while len(parts) > 1:
        parts = [a + b for a, b in zip(parts[::2], parts[1::2])]
    return parts[0]


def per_device(jacobian, residual, damping):
    sensors, spaces = lax.axis_size("sensor"), lax.axis_size("space")
    part, seen = jacobian.shape
    size = part * spaces
    span = seen // spaces
    me = lax.axis_index("space")
    both = ("sensor", "space")

    def swap(x, bits):
        return lax.ppermute(x, both, [(i, i ^ bits) for i in range(sensors * spaces)])

    def panel(step):
        return lax.dynamic_slice_in_dim(jacobian, (me ^ step) * span, span, 1)

    order = list(range(spaces // 2, spaces)) + list(range(1, spaces // 2))
    got = [swap(panel(step), step) for step in order]
    seen_residual = lax.dynamic_slice_in_dim(residual, me * span, span, 0).reshape(1, span)

    blocks = panel_starts(size)[-1]
    unit = 16 * sensors
    total = -(-(blocks + size // B) // unit) * unit
    half = total // 2
    quarter = half // sensors
    keep, send = pl.pallas_call(
        functools.partial(gram_kernel, order, total),
        out_shape=(f32(half, B), f32(half, B)),
        in_specs=[VMEM] * (spaces + 1),
        out_specs=(VMEM, VMEM),
        scratch_shapes=[pltpu.VMEM((size, span), jnp.float32), pltpu.VMEM((total, B), jnp.float32)],
        name="gram",
    )(seen_residual, panel(0), *got)
    pieces = pl.pallas_call(
        split_kernel,
        out_shape=[f32(quarter, B)] * sensors,
        in_specs=[VMEM] * 2,
        out_specs=[VMEM] * sensors,
        scratch_shapes=[pltpu.VMEM((half, B), jnp.float32)],
        name="split",
    )(keep, swap(send, spaces))
    plane = [(t >> 1) * 2 * spaces + (t & 1) for t in range(sensors)]
    mine = tree_sum([pieces[0]] + [swap(pieces[t], plane[t]) for t in range(1, sensors)])
    mine = tree_sum([mine] + [swap(mine, 2 * u) for u in range(1, spaces // 2)])
    mine = pl.pallas_call(
        join_kernel,
        out_shape=f32(half, B),
        in_specs=[VMEM] * sensors,
        out_specs=VMEM,
        name="join",
    )(mine, *[swap(mine, plane[t]) for t in range(1, sensors)])
    nb = size // B
    scratch = lambda rows: pltpu.VMEM((rows, B), jnp.float32)
    x = pl.pallas_call(
        functools.partial(solve_kernel, size),
        out_shape=f32(1, size),
        in_specs=[SMEM, VMEM, VMEM],
        out_specs=VMEM,
        scratch_shapes=[scratch(total), scratch(B), scratch(B)]
        + [scratch(size - k * B + 8) for k in range(nb)]
        + [scratch(size - (k + 1) * B + 8) for k in range(nb)],
        name="solve",
    )(damping, mine, swap(mine, spaces))
    return x.reshape(size)


def solution(mesh):
    placed = (P("space", "sensor"), P("sensor"), P())
    return jax.shard_map(per_device, mesh=mesh, in_specs=placed, out_specs=P(), check_vma=False)
```

time: 312 us -> 95.4 us (0.31)
  other arithmetic: 119 us -> 0.94 us
  blocking collectives: 58.5 us -> 0 us
  waiting for transfers between devices: 88.1 us -> 34.9 us
  Pallas kernels: 0 us -> 29.6 us
  starting transfers between devices: 0.04 us -> 22.9 us
  between operations: 16.9 us -> 0.77 us
  local copies, waits for them, and re-layouts: 19.7 us -> 6.07 us
  matrix products: 9.06 us -> 0 us
    another operation x17 -> x0, other arithmetic: 118 us -> none  [the longest x14 78.9 us: per_device(): factor = jnp.linalg.cholesky(damped)]
    psum x2 -> x0, waiting for transfers between devices: 88.1 us -> none  [the longest x1 77.3 us: per_device(): gram_group, grad_group = lax.psum((gram_local, grad_local), 'space')]
    ppermute x0 -> x18, waiting for transfers between devices: none -> 34.9 us  [swap(): lax.ppermute(x, both, [(i, i ^ bits) for i in range(sensors * spaces)])]
    all_to_all x1 -> x0, blocking collectives: 32.8 us -> none  [per_device(): lax.all_to_all(jacobian, 'space', split_axis=1, concat_axis=0, tiled=True)]
    pallas_call x0 -> x4, Pallas kernels: none -> 29.6 us  [the longest x1 20.5 us: per_device(): pl.pallas_call(functools.partial(solve_kernel, size), out_shape=f32(1, si...]
    psum x2 -> x0, blocking collectives: 25.7 us -> none  [the longest x1 20 us: per_device(): gram_group, grad_group = lax.psum((gram_local, grad_local), 'space')]
    ppermute x0 -> x18, starting transfers between devices: none -> 22.9 us  [swap(): lax.ppermute(x, both, [(i, i ^ bits) for i in range(sensors * spaces)])]
    another operation x34 -> x0, local copies, waits for them, and re-layouts: 9.14 us -> none
  transfers between devices with their start and end apart: 2 -> 18, of which waited for: 2 -> 13; matrix products, arithmetic and copies ran while one was open for 0% -> 1% of each run, Pallas kernels for 0% -> 0%
where the time goes in v1:
time: 95.4 us; the launch traced here: 95.1 us
  waiting for transfers between devices  34.9 us (37%)
  Pallas kernels  29.6 us (31%)
  starting transfers between devices  22.9 us (24%)
  local copies, waits for them, and re-layouts  6.07 us (6%)
    ppermute x18, waiting for transfers between devices, swap(): lax.ppermute(x, both, [(i, i ^ bits) for i in range(sensors * spaces)])  34.9 us
    ppermute x18, starting transfers between devices, swap(): lax.ppermute(x, both, [(i, i ^ bits) for i in range(sensors * spaces)])  22.9 us
    pallas_call x1, Pallas kernels, per_device(): pl.pallas_call(functools.partial(solve_kernel, size), out_shape=f32(1, si...  20.5 us
    pallas_call x1, Pallas kernels, per_device(): pl.pallas_call(functools.partial(gram_kernel, order, total), out_shape=(f...  5.42 us
    unnamed x26, local copies, waits for them, and re-layouts  2.72 us
    dynamic_slice x1, local copies, waits for them, and re-layouts, panel(): return lax.dynamic_slice_in_dim(jacobian, (me ^ step) * span, span, 1)  1.99 us
  transfers between devices with their start and end apart: 18, of which 13 were waited for; matrix products, arithmetic and copies ran while one was open for 1% of the time, Pallas kernels for 0%

profile of v1, /device:TPU:0, one launch (start us, length us, event | category | flops | bytes accessed | tf_op | source)
XLA Modules:
  0.0 95.1 jit_solution(3718130869203160042)
XLA Ops:
  0.0 2.0 %constant_dynamic-slice_fusion = (f32[64,512]{1,0:T(8,128)S(1)}, f32[64,512]{1,0:T(8,128)S(1)}, f32[64,512]{1,0:T(8,128)S(1)}, f32[64,512]{1,0:T(8,128)S(1)}, f3...) fusion(f32[64,4096]{1,0:T(8,128)} %param.3, s32[]{:T(128)S(6)} %select_n.32, ...), kind=kLoop, calls=%fused_computation.2 | loop fusion | bytes 2097184 | tf_op jit(solution)/shard_map/dynamic_slice | solution.py:185
  2.0 4.1 %collective-permute-start = (f32[64,512]{1,0:T(8,128)S(1)}, f32[64,512]{1,0:T(8,128)S(1)}, u32[]{:S(2)}, u32[]{:S(2)}) collective-permute-start(f32[64,512]{1,0:T(8,128)S(1)} %get-tuple-element.22), channel_id=1, source_target_pairs={{0,4},{1,5},{2,6},{3,7},{4,0},{5,1},{6,2},{7,3},{8,12},{9,13},{10,... | collective-permute-start | bytes 393224 | tf_op jit(solution)/shard_map/ppermute | solution.py:182
  6.1 1.3 %collective-permute-start.1 = (f32[64,512]{1,0:T(8,128)S(1)}, f32[64,512]{1,0:T(8,128)S(1)}, u32[]{:S(2)}, u32[]{:S(2)}) collective-permute-start(f32[64,512]{1,0:T(8,128)S(1)} %get-tuple-element.21), channel_id=1, source_target_pairs={{0,5},{1,4},{2,7},{3,6},{4,1},{5,0},{6,3},{7,2},{8,13},{9,12},{10,... | collective-permute-start | bytes 393224 | tf_op jit(solution)/shard_map/ppermute | solution.py:182
  7.3 3.6 %collective-permute-start.2 = (f32[64,512]{1,0:T(8,128)S(1)}, f32[64,512]{1,0:T(8,128)S(1)}, u32[]{:S(2)}, u32[]{:S(2)}) collective-permute-start(f32[64,512]{1,0:T(8,128)S(1)} %get-tuple-element.20), channel_id=1, source_target_pairs={{0,6},{1,7},{2,4},{3,5},{4,2},{5,3},{6,0},{7,1},{8,14},{9,15},{10,... | collective-permute-start | bytes 393224 | tf_op jit(solution)/shard_map/ppermute | solution.py:182
  10.9 1.7 %collective-permute-start.4 = (f32[64,512]{1,0:T(8,128)S(1)}, f32[64,512]{1,0:T(8,128)S(1)}, u32[]{:S(2)}, u32[]{:S(2)}) collective-permute-start(f32[64,512]{1,0:T(8,128)S(1)} %get-tuple-element.18), channel_id=1, source_target_pairs={{0,1},{1,0},{2,3},{3,2},{4,5},{5,4},{6,7},{7,6},{8,9},{9,8},{10,11... | collective-permute-start | bytes 393224 | tf_op jit(solution)/shard_map/ppermute | solution.py:182
  12.6 9.0 %collective-permute-done.refs_2_ = f32[64,512]{1,0:T(8,128)S(1)} collective-permute-done((f32[64,512]{1,0:T(8,128)S(1)}, f32[64,512]{1,0:T(8,128)S(1)}, u32[]{:S(2)}, u32[]{:S(2)}) %collective-permute-start) | collective-permute-done | bytes 131104 | tf_op jit(solution)/shard_map/ppermute | solution.py:182
  21.6 4.0 %collective-permute-done.1.refs_3_ = f32[64,512]{1,0:T(8,128)S(1)} collective-permute-done((f32[64,512]{1,0:T(8,128)S(1)}, f32[64,512]{1,0:T(8,128)S(1)}, u32[]{:S(2)}, u32[]{:S(2)}) %collective-permute-start.1) | collective-permute-done | bytes 131104 | tf_op jit(solution)/shard_map/ppermute | solution.py:182
  25.7 1.4 %dynamic_slice.27 = f32[512]{0:T(512)} dynamic-slice(f32[4096]{0:T(1024)} %param.4, s32[]{:T(128)S(6)} %select_n.25), dynamic_slice_sizes={512} | dynamic-slice | bytes 4100 | tf_op jit(solution)/shard_map/dynamic_slice | solution.py:189
  27.1 4.4 %collective-permute-done.6.refs_8_ = f32[64,512]{1,0:T(8,128)S(1)} collective-permute-done((f32[64,512]{1,0:T(8,128)S(1)}, f32[64,512]{1,0:T(8,128)S(1)}, u32[]{:S(2)}, u32[]{:S(2)}) %collective-permute-start.6) | collective-permute-done | bytes 131104 | tf_op jit(solution)/shard_map/ppermute | solution.py:182
  32.2 5.4 %gram.1 = (f32[672,128]{1,0:T(8,128)}, f32[672,128]{1,0:T(8,128)}) custom-call(f32[1,512]{1,0:T(1,128)} %bitcast.2, f32[64,512]{1,0:T(8,128)} %get-tuple-element.23.refs_1_, f32[64,512]{1,0:T(8,128)} %copy-done.3, f32[64,512]{1,0:T(8,128)} %copy-done.4, f32[64,512]{1,0:T(8,128)} %copy-done.5, f32[64,512]{1,0:T(8,128)} %copy-done.6, f32[64,512]{1,0:T(8,128)} %copy-done.7, ...), custom_call_target="tpu_custom_call" | custom-call | tf_op jit(solution)/shard_map/gram/pallas_call | solution.py:196
  37.6 1.9 %collective-permute-done.7.got_ref = f32[672,128]{1,0:T(8,128)S(1)} collective-permute-done((f32[672,128]{1,0:T(8,128)}, f32[672,128]{1,0:T(8,128)S(1)}, u32[]{:S(2)}, u32[]{:S(2)}) %collective-permute-start.7) | collective-permute-done | bytes 344096 | tf_op jit(solution)/shard_map/ppermute | solution.py:182
  40.2 1.9 %split.1 = (f32[168,128]{1,0:T(8,128)}, f32[168,128]{1,0:T(8,128)}, f32[168,128]{1,0:T(8,128)}, f32[168,128]{1,0:T(8,128)}) custom-call(f32[672,128]{1,0:T(8,128)} %get-tuple-element.11.keep_ref, f32[672,128]{1,0:T(8,128)} %copy-done), custom_call_target="tpu_custom_call" | custom-call | tf_op jit(solution)/shard_map/split/pallas_call | solution.py:204
  42.1 1.5 %collective-permute-start.10 = (f32[168,128]{1,0:T(8,128)}, f32[168,128]{1,0:T(8,128)S(1)}, u32[]{:S(2)}, u32[]{:S(2)}) collective-permute-start(f32[168,128]{1,0:T(8,128)} %get-tuple-element.16), channel_id=1, source_target_pairs={{0,17},{1,16},{2,19},{3,18},{4,21},{5,20},{6,23},{7,22},{8,25},{9,... | collective-permute-start | bytes 258056 | tf_op jit(solution)/shard_map/ppermute | solution.py:182
  43.6 1.5 %collective-permute-start.8 = (f32[168,128]{1,0:T(8,128)}, f32[168,128]{1,0:T(8,128)S(1)}, u32[]{:S(2)}, u32[]{:S(2)}) collective-permute-start(f32[168,128]{1,0:T(8,128)} %get-tuple-element.14), channel_id=1, source_target_pairs={{0,1},{1,0},{2,3},{3,2},{4,5},{5,4},{6,7},{7,6},{8,9},{9,8},{10,11... | collective-permute-start | bytes 258056 | tf_op jit(solution)/shard_map/ppermute | solution.py:182
  45.6 3.0 %collective-permute-done.10 = f32[168,128]{1,0:T(8,128)S(1)} collective-permute-done((f32[168,128]{1,0:T(8,128)}, f32[168,128]{1,0:T(8,128)S(1)}, u32[]{:S(2)}, u32[]{:S(2)}) %collective-permute-start.10) | collective-permute-done | bytes 86048 | tf_op jit(solution)/shard_map/ppermute | solution.py:182
  50.8 1.5 %collective-permute-start.11 = (f32[168,128]{1,0:T(8,128)S(1)}, f32[168,128]{1,0:T(8,128)S(1)}, u32[]{:S(2)}, u32[]{:S(2)}) collective-permute-start(f32[168,128]{1,0:T(8,128)S(1)} %add_add_fusion.1), channel_id=1, source_target_pairs={{0,2},{1,3},{2,0},{3,1},{4,6},{5,7},{6,4},{7,5},{8,10},{9,11},{10,... | collective-permute-start | bytes 258056 | tf_op jit(solution)/shard_map/ppermute | solution.py:182
  52.2 2.4 %collective-permute-start.12 = (f32[168,128]{1,0:T(8,128)S(1)}, f32[168,128]{1,0:T(8,128)S(1)}, u32[]{:S(2)}, u32[]{:S(2)}) collective-permute-start(f32[168,128]{1,0:T(8,128)S(1)} %add_add_fusion.1), channel_id=1, source_target_pairs={{0,4},{1,5},{2,6},{3,7},{4,0},{5,1},{6,2},{7,3},{8,12},{9,13},{10,... | collective-permute-start | bytes 258056 | tf_op jit(solution)/shard_map/ppermute | solution.py:182
  54.6 1.4 %collective-permute-start.13 = (f32[168,128]{1,0:T(8,128)S(1)}, f32[168,128]{1,0:T(8,128)S(1)}, u32[]{:S(2)}, u32[]{:S(2)}) collective-permute-start(f32[168,128]{1,0:T(8,128)S(1)} %add_add_fusion.1), channel_id=1, source_target_pairs={{0,6},{1,7},{2,4},{3,5},{4,2},{5,3},{6,0},{7,1},{8,14},{9,15},{10,... | collective-permute-start | bytes 258056 | tf_op jit(solution)/shard_map/ppermute | solution.py:182
  56.2 5.8 %collective-permute-done.12 = f32[168,128]{1,0:T(8,128)S(1)} collective-permute-done((f32[168,128]{1,0:T(8,128)S(1)}, f32[168,128]{1,0:T(8,128)S(1)}, u32[]{:S(2)}, u32[]{:S(2)}) %collective-permute-start.12) | collective-permute-done | bytes 86048 | tf_op jit(solution)/shard_map/ppermute | solution.py:182
  64.2 1.5 %collective-permute-start.16 = (f32[168,128]{1,0:T(8,128)S(1)}, f32[168,128]{1,0:T(8,128)S(1)}, u32[]{:S(2)}, u32[]{:S(2)}) collective-permute-start(f32[168,128]{1,0:T(8,128)S(1)} %add_add_fusion.refs_0_), channel_id=1, source_target_pairs={{0,17},{1,16},{2,19},{3,18},{4,21},{5,20},{6,23},{7,22},{8,25},{9,... | collective-permute-start | bytes 258056 | tf_op jit(solution)/shard_map/ppermute | solution.py:182
  67.7 1.9 %collective-permute-done.16.refs_3_ = f32[168,128]{1,0:T(8,128)S(1)} collective-permute-done((f32[168,128]{1,0:T(8,128)S(1)}, f32[168,128]{1,0:T(8,128)S(1)}, u32[]{:S(2)}, u32[]{:S(2)}) %collective-permute-start.16) | collective-permute-done | bytes 86048 | tf_op jit(solution)/shard_map/ppermute | solution.py:182
  70.2 1.8 %join.1.mine_ref = f32[672,128]{1,0:T(8,128)} custom-call(f32[168,128]{1,0:T(8,128)} %copy-done.2, f32[168,128]{1,0:T(8,128)} %copy-done.10, f32[168,128]{1,0:T(8,128)} %copy-done.11, f32[168,128]{1,0:T(8,128)} %copy-done.12), custom_call_target="tpu_custom_call" | custom-call | tf_op jit(solution)/shard_map/join/pallas_call | solution.py:215
  72.7 1.2 %collective-permute-done.17.other_ref = f32[672,128]{1,0:T(8,128)S(1)} collective-permute-done((f32[672,128]{1,0:T(8,128)}, f32[672,128]{1,0:T(8,128)S(1)}, u32[]{:S(2)}, u32[]{:S(2)}) %collective-permute-start.17) | collective-permute-done | bytes 344096 | tf_op jit(solution)/shard_map/ppermute | solution.py:182
  74.6 20.5 %solve.1 = f32[1,512]{1,0:T(1,128)} custom-call(f32[1]{0:T(128)S(6)} %copy.4.damp_ref, f32[672,128]{1,0:T(8,128)} %join.1.mine_ref, f32[672,128]{1,0:T(8,128)} %copy-done.1), custom_call_target="tpu_custom_call" | custom-call | tf_op jit(solution)/shard_map/solve/pallas_call | solution.py:224
  (46 shorter events, 9.9 us)
Async XLA Ops:
  2.0 19.6 %collective-permute-start = (f32[64,512]{1,0:T(8,128)S(1)}, f32[64,512]{1,0:T(8,128)S(1)}, u32[]{:S(2)}, u32[]{:S(2)}) collective-permute-start(f32[64,512]{1,0:T(8,128)S(1)} %get-tuple-element.22), channel_id=1, source_target_pairs={{0,4},{1,5},{2,6},{3,7},{4,0},{5,1},{6,2},{7,3},{8,12},{9,13},{10,... | collective-permute-start | bytes 393224 | tf_op jit(solution)/shard_map/ppermute | solution.py:182
  6.1 19.6 %collective-permute-start.1 = (f32[64,512]{1,0:T(8,128)S(1)}, f32[64,512]{1,0:T(8,128)S(1)}, u32[]{:S(2)}, u32[]{:S(2)}) collective-permute-start(f32[64,512]{1,0:T(8,128)S(1)} %get-tuple-element.21), channel_id=1, source_target_pairs={{0,5},{1,4},{2,7},{3,6},{4,1},{5,0},{6,3},{7,2},{8,13},{9,12},{10,... | collective-permute-start | bytes 393224 | tf_op jit(solution)/shard_map/ppermute | solution.py:182
  7.3 19.7 %collective-permute-start.2 = (f32[64,512]{1,0:T(8,128)S(1)}, f32[64,512]{1,0:T(8,128)S(1)}, u32[]{:S(2)}, u32[]{:S(2)}) collective-permute-start(f32[64,512]{1,0:T(8,128)S(1)} %get-tuple-element.20), channel_id=1, source_target_pairs={{0,6},{1,7},{2,4},{3,5},{4,2},{5,3},{6,0},{7,1},{8,14},{9,15},{10,... | collective-permute-start | bytes 393224 | tf_op jit(solution)/shard_map/ppermute | solution.py:182
  10.9 16.1 %collective-permute-start.3 = (f32[64,512]{1,0:T(8,128)S(1)}, f32[64,512]{1,0:T(8,128)S(1)}, u32[]{:S(2)}, u32[]{:S(2)}) collective-permute-start(f32[64,512]{1,0:T(8,128)S(1)} %get-tuple-element.19), channel_id=1, source_target_pairs={{0,7},{1,6},{2,5},{3,4},{4,3},{5,2},{6,1},{7,0},{8,15},{9,14},{10,... | collective-permute-start | bytes 393224 | tf_op jit(solution)/shard_map/ppermute | solution.py:182
  10.9 16.1 %collective-permute-start.4 = (f32[64,512]{1,0:T(8,128)S(1)}, f32[64,512]{1,0:T(8,128)S(1)}, u32[]{:S(2)}, u32[]{:S(2)}) collective-permute-start(f32[64,512]{1,0:T(8,128)S(1)} %get-tuple-element.18), channel_id=1, source_target_pairs={{0,1},{1,0},{2,3},{3,2},{4,5},{5,4},{6,7},{7,6},{8,9},{9,8},{10,11... | collective-permute-start | bytes 393224 | tf_op jit(solution)/shard_map/ppermute | solution.py:182
  21.6 9.9 %copy-start.3 = (f32[64,512]{1,0:T(8,128)}, f32[64,512]{1,0:T(8,128)S(1)}, u32[]{:S(2)}) copy-start(f32[64,512]{1,0:T(8,128)S(1)} %collective-permute-done.refs_2_) | copy-start | bytes 393220
  21.6 5.5 %collective-permute-start.5 = (f32[64,512]{1,0:T(8,128)S(1)}, f32[64,512]{1,0:T(8,128)S(1)}, u32[]{:S(2)}, u32[]{:S(2)}) collective-permute-start(f32[64,512]{1,0:T(8,128)S(1)} %get-tuple-element.24), channel_id=1, source_target_pairs={{0,2},{1,3},{2,0},{3,1},{4,6},{5,7},{6,4},{7,5},{8,10},{9,11},{10,... | collective-permute-start | bytes 393224 | tf_op jit(solution)/shard_map/ppermute | solution.py:182
  25.7 5.9 %copy-start.4 = (f32[64,512]{1,0:T(8,128)}, f32[64,512]{1,0:T(8,128)S(1)}, u32[]{:S(2)}) copy-start(f32[64,512]{1,0:T(8,128)S(1)} %collective-permute-done.1.refs_3_) | copy-start | bytes 393220
  25.7 5.9 %collective-permute-start.6 = (f32[64,512]{1,0:T(8,128)S(1)}, f32[64,512]{1,0:T(8,128)S(1)}, u32[]{:S(2)}, u32[]{:S(2)}) collective-permute-start(f32[64,512]{1,0:T(8,128)S(1)} %get-tuple-element.17), channel_id=1, source_target_pairs={{0,3},{1,2},{2,1},{3,0},{4,7},{5,6},{6,5},{7,4},{8,11},{9,10},{10,... | collective-permute-start | bytes 393224 | tf_op jit(solution)/shard_map/ppermute | solution.py:182
  27.1 4.5 %copy-start.5 = (f32[64,512]{1,0:T(8,128)}, f32[64,512]{1,0:T(8,128)S(1)}, u32[]{:S(2)}) copy-start(f32[64,512]{1,0:T(8,128)S(1)} %collective-permute-done.2.refs_4_) | copy-start | bytes 393220
  27.1 4.5 %copy-start.6 = (f32[64,512]{1,0:T(8,128)}, f32[64,512]{1,0:T(8,128)S(1)}, u32[]{:S(2)}) copy-start(f32[64,512]{1,0:T(8,128)S(1)} %collective-permute-done.3.refs_5_) | copy-start | bytes 393220
  27.1 4.5 %copy-start.7 = (f32[64,512]{1,0:T(8,128)}, f32[64,512]{1,0:T(8,128)S(1)}, u32[]{:S(2)}) copy-start(f32[64,512]{1,0:T(8,128)S(1)} %collective-permute-done.4.refs_6_) | copy-start | bytes 393220
  37.6 1.9 %collective-permute-start.7 = (f32[672,128]{1,0:T(8,128)}, f32[672,128]{1,0:T(8,128)S(1)}, u32[]{:S(2)}, u32[]{:S(2)}) collective-permute-start(f32[672,128]{1,0:T(8,128)} %get-tuple-element.12), channel_id=1, source_target_pairs={{0,8},{1,9},{2,10},{3,11},{4,12},{5,13},{6,14},{7,15},{8,0},{9,1},... | collective-permute-start | bytes 1032200 | tf_op jit(solution)/shard_map/ppermute | solution.py:182
  42.1 6.5 %collective-permute-start.10 = (f32[168,128]{1,0:T(8,128)}, f32[168,128]{1,0:T(8,128)S(1)}, u32[]{:S(2)}, u32[]{:S(2)}) collective-permute-start(f32[168,128]{1,0:T(8,128)} %get-tuple-element.16), channel_id=1, source_target_pairs={{0,17},{1,16},{2,19},{3,18},{4,21},{5,20},{6,23},{7,22},{8,25},{9,... | collective-permute-start | bytes 258056 | tf_op jit(solution)/shard_map/ppermute | solution.py:182
  43.6 6.1 %collective-permute-start.8 = (f32[168,128]{1,0:T(8,128)}, f32[168,128]{1,0:T(8,128)S(1)}, u32[]{:S(2)}, u32[]{:S(2)}) collective-permute-start(f32[168,128]{1,0:T(8,128)} %get-tuple-element.14), channel_id=1, source_target_pairs={{0,1},{1,0},{2,3},{3,2},{4,5},{5,4},{6,7},{7,6},{8,9},{9,8},{10,11... | collective-permute-start | bytes 258056 | tf_op jit(solution)/shard_map/ppermute | solution.py:182
  45.1 4.8 %collective-permute-start.9 = (f32[168,128]{1,0:T(8,128)}, f32[168,128]{1,0:T(8,128)S(1)}, u32[]{:S(2)}, u32[]{:S(2)}) collective-permute-start(f32[168,128]{1,0:T(8,128)} %get-tuple-element.15), channel_id=1, source_target_pairs={{0,16},{1,17},{2,18},{3,19},{4,20},{5,21},{6,22},{7,23},{8,24},{9,... | collective-permute-start | bytes 258056 | tf_op jit(solution)/shard_map/ppermute | solution.py:182
  50.8 5.5 %collective-permute-start.11 = (f32[168,128]{1,0:T(8,128)S(1)}, f32[168,128]{1,0:T(8,128)S(1)}, u32[]{:S(2)}, u32[]{:S(2)}) collective-permute-start(f32[168,128]{1,0:T(8,128)S(1)} %add_add_fusion.1), channel_id=1, source_target_pairs={{0,2},{1,3},{2,0},{3,1},{4,6},{5,7},{6,4},{7,5},{8,10},{9,11},{10,... | collective-permute-start | bytes 258056 | tf_op jit(solution)/shard_map/ppermute | solution.py:182
  52.2 9.8 %collective-permute-start.12 = (f32[168,128]{1,0:T(8,128)S(1)}, f32[168,128]{1,0:T(8,128)S(1)}, u32[]{:S(2)}, u32[]{:S(2)}) collective-permute-start(f32[168,128]{1,0:T(8,128)S(1)} %add_add_fusion.1), channel_id=1, source_target_pairs={{0,4},{1,5},{2,6},{3,7},{4,0},{5,1},{6,2},{7,3},{8,12},{9,13},{10,... | collective-permute-start | bytes 258056 | tf_op jit(solution)/shard_map/ppermute | solution.py:182
  54.6 7.4 %collective-permute-start.13 = (f32[168,128]{1,0:T(8,128)S(1)}, f32[168,128]{1,0:T(8,128)S(1)}, u32[]{:S(2)}, u32[]{:S(2)}) collective-permute-start(f32[168,128]{1,0:T(8,128)S(1)} %add_add_fusion.1), channel_id=1, source_target_pairs={{0,6},{1,7},{2,4},{3,5},{4,2},{5,3},{6,0},{7,1},{8,14},{9,15},{10,... | collective-permute-start | bytes 258056 | tf_op jit(solution)/shard_map/ppermute | solution.py:182
  62.1 7.5 %copy-start.2 = (f32[168,128]{1,0:T(8,128)}, f32[168,128]{1,0:T(8,128)S(1)}, u32[]{:S(2)}) copy-start(f32[168,128]{1,0:T(8,128)S(1)} %add_add_fusion.refs_0_) | copy-start | bytes 258052
  62.1 4.6 %collective-permute-start.14 = (f32[168,128]{1,0:T(8,128)S(1)}, f32[168,128]{1,0:T(8,128)S(1)}, u32[]{:S(2)}, u32[]{:S(2)}) collective-permute-start(f32[168,128]{1,0:T(8,128)S(1)} %add_add_fusion.refs_0_), channel_id=1, source_target_pairs={{0,1},{1,0},{2,3},{3,2},{4,5},{5,4},{6,7},{7,6},{8,9},{9,8},{10,11... | collective-permute-start | bytes 258056 | tf_op jit(solution)/shard_map/ppermute | solution.py:182
  63.2 4.5 %collective-permute-start.15 = (f32[168,128]{1,0:T(8,128)S(1)}, f32[168,128]{1,0:T(8,128)S(1)}, u32[]{:S(2)}, u32[]{:S(2)}) collective-permute-start(f32[168,128]{1,0:T(8,128)S(1)} %add_add_fusion.refs_0_), channel_id=1, source_target_pairs={{0,16},{1,17},{2,18},{3,19},{4,20},{5,21},{6,22},{7,23},{8,24},{9,... | collective-permute-start | bytes 258056 | tf_op jit(solution)/shard_map/ppermute | solution.py:182
  64.2 5.4 %collective-permute-start.16 = (f32[168,128]{1,0:T(8,128)S(1)}, f32[168,128]{1,0:T(8,128)S(1)}, u32[]{:S(2)}, u32[]{:S(2)}) collective-permute-start(f32[168,128]{1,0:T(8,128)S(1)} %add_add_fusion.refs_0_), channel_id=1, source_target_pairs={{0,17},{1,16},{2,19},{3,18},{4,21},{5,20},{6,23},{7,22},{8,25},{9,... | collective-permute-start | bytes 258056 | tf_op jit(solution)/shard_map/ppermute | solution.py:182
  72.0 1.9 %collective-permute-start.17 = (f32[672,128]{1,0:T(8,128)}, f32[672,128]{1,0:T(8,128)S(1)}, u32[]{:S(2)}, u32[]{:S(2)}) collective-permute-start(f32[672,128]{1,0:T(8,128)} %join.1.mine_ref), channel_id=1, source_target_pairs={{0,8},{1,9},{2,10},{3,11},{4,12},{5,13},{6,14},{7,15},{8,0},{9,1},... | collective-permute-start | bytes 1032200 | tf_op jit(solution)/shard_map/ppermute | solution.py:182
  (7 other events, 12.0 us)
